TPU v7x, 32 devices: a whole 2x2x4 slice. The times are simulated.
32 devices in a mesh: pipe: 4 (over y, core), ctx: 4 (over z), dp: 2 (over x).
Axes of the slice: x: 2, y: 2, z: 4, core: 2. Of those that a mesh axis runs over, the one named last changes fastest.
Arguments:
- hidden: bfloat16 [4, 1024, 4096], P('pipe', 'ctx', 'dp'), may hold values from -64 to 64
- cotangent: bfloat16 [4, 1024, 4096], P('pipe', 'ctx', 'dp'), may hold values from -6 to 6
- gain_rows: float32 [4, 4096], P('pipe', ('dp', 'ctx')), may hold values from 0.5 to 1.5
- short_taps: float32 [4, 9, 4096], P('pipe', None, ('dp', 'ctx')), may hold values from -3.5 to 3.5
- long_taps: float32 [4, 7, 4096], P('pipe', None, ('dp', 'ctx')), may hold values from -2 to 2
Outputs:
- hidden_grad: bfloat16 [4, 1024, 4096], P('pipe', 'ctx', 'dp')
- gain_grad: float32 [4, 4096], P('pipe', ('dp', 'ctx'))
- short_grad: float32 [4, 9, 4096], P('pipe', None, ('dp', 'ctx'))
- long_grad: float32 [4, 7, 4096], P('pipe', None, ('dp', 'ctx'))
All inputs are finite; a program needn't handle non-finite values.
Results may differ from a plain program's by a relative error of at most 0.0056.
Values may be sent and summed in bfloat16 or wider, within the bound.
A program may use at most 64 MiB of HBM per device.

v0:
```python
import jax
import jax.numpy as jnp
from jax import lax
from jax.sharding import PartitionSpec as P

WIDTH = 4096


def passed_along(value, axis, steps):
    count = lax.axis_size(axis)
    initial, last = (max(0, -steps), min(count, count - steps))
    return lax.ppermute(value, axis, [(source, source + steps) for source in range(initial, last)])


def shifted(value, axis, steps):
    count = lax.axis_size(axis)
    pairs = [(source, (source + steps) % count) for source in range(count)]
    return lax.ppermute(value, axis, pairs)


def delayed(source, places):
    if places == 0:
        return source
    zero_rows = jnp.zeros(source.shape[:-2] + (places, source.shape[-1]), source.dtype)
    return jnp.concatenate([zero_rows, source[..., : source.shape[-2] - places, :]], axis=-2)


def conv_branch(normed, short_filter, long_filter):
    tap_count = short_filter.shape[0] // 3
    lagged = [delayed(normed, tap_index) for tap_index in range(tap_count)]
    streams = []
    for stream_index in range(3):
        summed = short_filter[tap_count * stream_index] * lagged[0]
        for tap_index in range(1, tap_count):
            summed = summed + short_filter[tap_count * stream_index + tap_index] * lagged[tap_index]
        streams.append(summed)
    product = streams[1] * streams[2]
    mixing = long_filter[0] * product
    for tap_index in range(1, long_filter.shape[0]):
        mixing = mixing + long_filter[tap_index] * delayed(product, tap_index)
    return streams[0] * mixing


def row_total(values):
    return lax.psum(values, "dp")


def block_forward(values, filter_set):
    squares = row_total(jnp.sum(values * values, axis=-1))
    scale = lax.rsqrt(squares / WIDTH + 1e-05)[:, None]
    normed = values * scale * filter_set[0]
    branch, pull = jax.vjp(conv_branch, normed, filter_set[1], filter_set[2])
    return (values + branch, (values, scale, pull))


def block_backward(saved, filter_set, upstream):
    values, scale, pull = saved
    normed_grad, short_grad, long_grad = pull(upstream)
    gain_grad = jnp.sum(values * scale * normed_grad, axis=0)
    weighted = filter_set[0] * normed_grad
    projected = row_total(jnp.sum(values * weighted, axis=-1))[:, None]
    values_grad = upstream + scale * weighted - values * (scale * scale * scale / WIDTH) * projected
    return (values_grad, (gain_grad, short_grad, long_grad))


def pad_top(values, total_rows):
    zero_rows = jnp.zeros((total_rows - values.shape[0], values.shape[1]), values.dtype)
    return jnp.concatenate([zero_rows, values], axis=0)


def rows_across(values):
    return passed_along(values, "ctx", 1)


def grads_across(values):
    return passed_along(values, "ctx", -1)


def pipe_half(values, offset):
    return shifted(values, "pipe", offset)


def pipe_full(values, offset):
    return shifted(values, "pipe", offset)


def unpack_rows(filter_rows, short_count):
    return (filter_rows[0], filter_rows[1 : 1 + short_count], filter_rows[1 + short_count :])


def pack_rows(filter_set):
    return jnp.concatenate([filter_set[0][None, :], filter_set[1], filter_set[2]], axis=0)


def add_returned(local_grad, returned, depth):
    row_count = local_grad.shape[0] - depth
    zero_rows = jnp.zeros((row_count - depth, local_grad.shape[1]), jnp.float32)
    return local_grad[depth:] + jnp.concatenate([zero_rows, returned], axis=0)


def per_device(hidden, cotangent, gain_rows, short_taps, long_taps):
    row_count = hidden.shape[1]
    short_count = short_taps.shape[1]
    reach = short_count // 3 + long_taps.shape[1] - 2
    signal = hidden[0]
    cot_local = cotangent[0]
    packed = jnp.concatenate([gain_rows, short_taps[0], long_taps[0]], axis=0)
    filters = lax.all_gather(packed, "ctx", axis=1, tiled=True)
    first_filters = unpack_rows(filters, short_count)
    rim_rows = rows_across(signal[row_count - reach :]).astype(jnp.float32)
    signal_ext = jnp.concatenate([rim_rows, signal.astype(jnp.float32)], axis=0)
    first_out, first_saved = block_forward(signal_ext, first_filters)
    inner = first_out[signal_ext.shape[0] - row_count :].astype(jnp.bfloat16)
    arrived = pipe_half(inner, 1)
    inner_rim = rows_across(arrived[row_count - reach :]).astype(jnp.float32)
    second_ext = jnp.concatenate([inner_rim, arrived.astype(jnp.float32)], axis=0)
    second_out, second_saved = block_forward(second_ext, first_filters)
    second_up = pad_top(cot_local.astype(jnp.float32), second_ext.shape[0])
    inner_grad_ext, second_grads = block_backward(second_saved, first_filters, second_up)
    returned = grads_across(inner_grad_ext[:reach])
    inner_grad = add_returned(inner_grad_ext, returned, reach)
    inner_grad = pipe_full(inner_grad, -1)
    first_up = pad_top(inner_grad, signal_ext.shape[0])
    signal_grad_ext, first_grads = block_backward(first_saved, first_filters, first_up)
    returned_signal = grads_across(signal_grad_ext[:reach])
    hidden_grad = add_returned(signal_grad_ext, returned_signal, reach).astype(jnp.bfloat16)
    summed_grads = pack_rows(first_grads) + pack_rows(second_grads)
    reduced = lax.psum_scatter(summed_grads, "ctx", scatter_dimension=1, tiled=True)
    gain_grad = reduced[0:1]
    short_grad = reduced[1 : 1 + short_count][None]
    long_grad = reduced[1 + short_count :][None]
    return (hidden_grad[None], gain_grad, short_grad, long_grad)


def solution(mesh):
    in_specs = (
        P("pipe", "ctx", "dp"),
        P("pipe", "ctx", "dp"),
        P("pipe", ("dp", "ctx")),
        P("pipe", None, ("dp", "ctx")),
        P("pipe", None, ("dp", "ctx")),
    )
    out_specs = (
        P("pipe", "ctx", "dp"),
        P("pipe", ("dp", "ctx")),
        P("pipe", None, ("dp", "ctx")),
        P("pipe", None, ("dp", "ctx")),
    )
    return jax.shard_map(
        per_device, mesh=mesh, in_specs=in_specs, out_specs=out_specs, check_vma=False
    )
```

profile of v0, /device:TPU:0, one launch (start us, length us, event | category | flops | bytes accessed | tf_op | source)
XLA Modules:
  0.0 188.0 jit_solution(3203681902151841099)
XLA Ops:
  7.2 0.8 slice_bitcast_fusion
  8.1 4.9 %collective-permute-start = (bf16[8,2048]{1,0:T(8,128)(2,1)S(1)}, bf16[8,2048]{1,0:T(8,128)(2,1)S(1)}, u32[]{:S(2)}, u32[]{:S(2)}) collective-permute-start(bf16[8,2048]{1,0:T(8,128)(2,1)S(1)} %slice_bitcast_fusion), channel_id=1, source_target_pairs={{0,2},{2,4},{4,6},{1,3},{3,5},{5,7},{8,10},{10,12},{12,14},{9,11},... | collective-permute-start | bytes 98312 | tf_op jit(solution)/shard_map/ppermute | solution.py:12
  13.0 0.7 copy.14
  13.7 0.7 copy.13
  14.4 0.7 pad_maximum_fusion.2
  15.1 14.3 %all_gather.3 = f32[17,2048]{1,0:T(8,128)S(1)} all-gather(f32[17,512]{1,0:T(8,128)S(1)} %pad_maximum_fusion.2), channel_id=1, replica_groups=mesh['pipe'=4,'ctx'=4,'dp'=2] {'ctx'}, dimensions={1}, use_global_device_ids=true | all-gather | bytes 174080 | tf_op jit(solution)/shard_map/all_gather | solution.py:108
  29.5 1.5 multiply_reduce_fusion.34
  31.0 4.9 %psum.28 = f32[264]{0:T(512)S(1)} all-reduce(f32[264]{0:T(512)S(1)} %multiply_reduce_fusion.34), channel_id=1, replica_groups=mesh['pipe'=4,'ctx'=4,'dp'=2] {'dp'}, use_global_device_ids=true, to_apply=%region_1.0 | all-reduce | flops 264 | bytes 2112 | tf_op jit(solution)/shard_map/psum | solution.py:45
  36.0 0.6 fusion.20
  36.8 1.7 multiply_add_fusion.7
  38.6 2.0 %multiply_add_fusion.4 = f32[264,2048]{1,0:T(8,128)S(1)} fusion(f32[264,2048]{1,0:T(8,128)S(1)} %get-tuple-element.51, f32[258,2048]{1,0:T(8,128)S(1)} %bitcast.91, f32[259,2048]{1,0:T(8,128)S(1)} %bitcast.92, f32[260,2048]{1,0:T(8,128)S(1)} %bitcast.93, f32[261,2048]{1,0:T(8,128)S(1)} %bitcast.94, f32[262,2048]{1,0:T(8,128)S(1)} %bitcast.95, ...), kind=kLoop, calls=%fused_computation.87 | loop fusion | flops 7028736 | bytes 17186816 | tf_op jit(solution)/shard_map/jvp()/add | solution.py:40
  40.9 0.6 fusion.17
  41.9 14.2 %collective-permute-done.1 = bf16[256,2048]{1,0:T(8,128)(2,1)S(1)} collective-permute-done((bf16[256,2048]{1,0:T(8,128)(2,1)S(1)}, bf16[256,2048]{1,0:T(8,128)(2,1)S(1)}, u32[]{:S(2)}, u32[]{:S(2)}) %collective-permute-start.1) | collective-permute-done | bytes 1048608 | tf_op jit(solution)/shard_map/ppermute | solution.py:18
  56.2 1.3 collective-permute-start.2
  57.4 1.6 collective-permute-done.2
  59.3 5.1 %psum.29 = f32[264]{0:T(512)S(1)} all-reduce(f32[264]{0:T(512)S(1)} %fusion.4), channel_id=1, replica_groups=mesh['pipe'=4,'ctx'=4,'dp'=2] {'dp'}, use_global_device_ids=true, to_apply=%region_3.0 | all-reduce | flops 264 | bytes 2112 | tf_op jit(solution)/shard_map/psum | solution.py:45
  64.8 1.4 fusion.24
  66.1 4.7 %multiply_reduce_fusion.6 = (f32[2048]{0:T(1024)S(1)}, f32[2048]{0:T(1024)S(1)}, f32[2048]{0:T(1024)S(1)}, f32[2048]{0:T(1024)S(1)}, f32[2048]{0:T(1024)S(1)}, /...) fusion(f32[258,2048]{1,0:T(8,128)S(1)} %bitcast.79, f32[264,2048]{1,0:T(8,128)S(1)} %fusion.24, ...), kind=kLoop, calls=%fused_computation.52 | loop fusion | flops 14583808 | bytes 23651360 | tf_op jit(solution)/shard_map/transpose(jvp())/reduce_sum | solution.py:40
  73.0 6.8 %multiply_reduce_fusion.15 = (f32[2048]{0:T(1024)S(1)}, f32[2048]{0:T(1024)S(1)}, f32[2048]{0:T(1024)S(1)}, f32[2048]{0:T(1024)S(1)}, f32[2048]{0:T(1024)}, /*in...) fusion(f32[262,2048]{1,0:T(8,128)S(1)} %bitcast.107, ...), kind=kLoop, calls=%fused_computation.61 | loop fusion | flops 31340544 | bytes 43041824 | tf_op jit(solution)/shard_map/transpose(jvp())/reduce_sum | solution.py:35
  79.8 0.8 fusion.11
  80.6 0.9 fusion.13
  81.5 2.5 %fusion.2 = (f32[2048]{0:T(1024)S(1)}, f32[264]{0:T(512)S(1)}, f32[264,2048]{1,0:T(8,128)}) fusion(f32[264]{0:T(512)S(1)} %get-tuple-element.72, bf16[256,2048]{1,0:T(8,128)(2,1)S(1)} %collective-permute-done.1, bf16[8,2048]{1,0:T(8,128)(2,1)S(1)} %collective-permute-done.2, f32[2048]{0:T(1024)S(1)} %bitcast.129, f32[263,2048]{1,0:T(8,128)S(1)} %fusion.11, ...), kind=kLoop, calls=%fused_computation.9 | loop fusion | flops 9189112 | bytes 14075968 | tf_op jit(solution)/shard_map/reduce_sum | solution.py:59
  84.0 4.9 %psum.30 = f32[264]{0:T(512)S(1)} all-reduce(f32[264]{0:T(512)S(1)} %get-tuple-element.5), channel_id=1, replica_groups=mesh['pipe'=4,'ctx'=4,'dp'=2] {'dp'}, use_global_device_ids=true, to_apply=%region_5.0 | all-reduce | flops 264 | bytes 2112 | tf_op jit(solution)/shard_map/psum | solution.py:45
  89.0 2.5 %fusion.3 = f32[264,2048]{1,0:T(8,128)S(1)} fusion(f32[264,2048]{1,0:T(8,128)} %get-tuple-element.49, f32[264]{0:T(512)S(1)} %psum.30, f32[264]{0:T(512)S(1)} %get-tuple-element.71, f32[264]{0:T(512)S(1)} %get-tuple-element.72, f32[2048]{0:T(1024)S(1)} %bitcast.130, bf16[256,2048]{1,0:T(8,128)(2,1)} %bitcast.120, ...), kind=kLoop, calls=%fused_computation.10 | loop fusion | flops 5947392 | bytes 6466656 | tf_op jit(solution)/shard_map/sub | solution.py:62
  91.5 1.4 collective-permute-start.3
  92.9 5.2 %collective-permute-done.3 = f32[8,2048]{1,0:T(8,128)S(1)} collective-permute-done((f32[8,2048]{1,0:T(8,128)S(1)}, f32[8,2048]{1,0:T(8,128)S(1)}, u32[]{:S(2)}, u32[]{:S(2)}) %collective-permute-start.3) | collective-permute-done | bytes 65568 | tf_op jit(solution)/shard_map/ppermute | solution.py:12
  98.5 23.5 %collective-permute-done.4 = f32[256,2048]{1,0:T(8,128)S(1)} collective-permute-done((f32[256,2048]{1,0:T(8,128)S(1)}, f32[256,2048]{1,0:T(8,128)S(1)}, u32[]{:S(2)}, u32[]{:S(2)}) %collective-permute-start.4) | collective-permute-done | bytes 2097184 | tf_op jit(solution)/shard_map/ppermute | solution.py:18
  122.1 2.6 %multiply_reduce_fusion.22 = (f32[2048]{0:T(1024)S(1)}, f32[2048]{0:T(1024)S(1)}, f32[2048]{0:T(1024)S(1)}, f32[2048]{0:T(1024)S(1)}, f32[2048]{0:T(1024)S(1)}, ...) fusion(f32[258,2048]{1,0:T(8,128)S(1)} %bitcast.97, f32[264,2048]{1,0:T(8,128)S(1)} %get-tuple-element.51, ...), kind=kLoop, calls=%fused_computation.68 | loop fusion | flops 8095744 | bytes 21446656 | tf_op jit(solution)/shard_map/transpose(jvp())/reduce_sum | solution.py:40
  125.8 1.8 slice_multiply_fusion.9
  127.5 1.8 slice_multiply_fusion.10
  129.3 1.8 slice_multiply_fusion.11
  132.0 7.2 %multiply_reduce_fusion.31 = (f32[2048]{0:T(1024)S(1)}, f32[2048]{0:T(1024)S(1)}, f32[2048]{0:T(1024)S(1)}, f32[2048]{0:T(1024)S(1)}, f32[2048]{0:T(1024)S(1)}, ...) fusion(f32[262,2048]{1,0:T(8,128)S(1)} %bitcast.111, ...), kind=kLoop, calls=%fused_computation.77 | loop fusion | flops 23771136 | bytes 31237152 | tf_op jit(solution)/shard_map/transpose(jvp())/reduce_sum | solution.py:35
  139.2 0.8 fusion.7
  140.0 0.8 fusion.9
  140.9 2.6 %multiply_reduce_fusion.32 = (f32[2048]{0:T(1024)S(1)}, f32[264]{0:T(512)S(1)}, f32[264,2048]{1,0:T(8,128)}) fusion(f32[264]{0:T(512)S(1)} %get-tuple-element.70, bf16[256,2048]{1,0:T(8,128)(2,1)S(1)} %bitcast.118, bf16[8,2048]{1,0:T(8,128)(2,1)S(1)} %collective-permute-done, f32[2048]{0:T(1024)S(1)} %bitcast.132, f32[263,2048]{1,0:T(8,128)S(1)} %fusion.7, ...), kind=kLoop, calls=%fused_computation.78 | loop fusion | flops 9189112 | bytes 14075968 | tf_op jit(solution)/shard_map/reduce_sum | solution.py:59
  143.4 4.9 %psum.31 = f32[264]{0:T(512)S(1)} all-reduce(f32[264]{0:T(512)S(1)} %get-tuple-element.7), channel_id=1, replica_groups=mesh['pipe'=4,'ctx'=4,'dp'=2] {'dp'}, use_global_device_ids=true, to_apply=%region_7.0 | all-reduce | flops 264 | bytes 2112 | tf_op jit(solution)/shard_map/psum | solution.py:45
  148.4 2.3 %multiply_subtract_fusion = f32[264,2048]{1,0:T(8,128)S(1)} fusion(f32[264,2048]{1,0:T(8,128)} %get-tuple-element.48, f32[256,2048]{1,0:T(8,128)S(1)} %copy-done.9, f32[264]{0:T(512)S(1)} %psum.31, f32[264]{0:T(512)S(1)} %copy-done.20, f32[2048]{0:T(1024)S(1)} %bitcast.133, f32[264]{0:T(512)S(1)} %get-tuple-element.70, bf16[256,2048]{1,0:T(8,128)(2,1)S(1)} %bitcast.119, ...), kind=kLoop, calls=%fused_computation.79 | loop fusion | flops 5406720 | bytes 7515232 | tf_op jit(solution)/shard_map/sub | solution.py:62
  150.7 1.3 copy-done.11
  152.0 1.3 collective-permute-start.5
  153.8 0.8 maximum_add_fusion
  154.5 4.3 %collective-permute-done.5 = f32[8,2048]{1,0:T(8,128)S(1)} collective-permute-done((f32[8,2048]{1,0:T(8,128)S(1)}, f32[8,2048]{1,0:T(8,128)S(1)}, u32[]{:S(2)}, u32[]{:S(2)}) %collective-permute-start.5) | collective-permute-done | bytes 65568 | tf_op jit(solution)/shard_map/ppermute | solution.py:12
  158.8 2.7 %fusion.18 = bf16[1,256,2048]{2,1,0:T(8,128)(2,1)} fusion(f32[8,2048]{1,0:T(8,128)S(1)} %collective-permute-done.5, f32[264,2048]{1,0:T(8,128)} %copy-done.11), kind=kLoop, calls=%fused_computation.104 | loop fusion | flops 1048576 | bytes 3211264 | tf_op jit(solution)/shard_map/broadcast_in_dim | solution.py:132
  161.6 15.5 %reduce-scatter.2.cloned.1.call-done = f32[17,512]{1,0:T(8,128)} async-done(((f32[17,2048]{1,0:T(8,128)}), f32[17,512]{1,0:T(8,128)}) %reduce-scatter.2.cloned.1.call-update) | async-done | bytes 34832 | tf_op jit(solution)/shard_map/reduce_scatter | solution.py:128
  177.1 0.8 slice.253
  177.9 0.6 broadcast_in_dim.13
  178.5 0.8 slice.254
  179.3 0.6 broadcast_in_dim.14
  179.9 1.3 slice.252
  (67 shorter events, 6.6 us)
Async XLA Ops:
  7.2 29.4 %copy-start.2 = (bf16[1,256,2048]{2,1,0:T(8,128)(2,1)S(1)}, bf16[1,256,2048]{2,1,0:T(8,128)(2,1)}, u32[]{:S(2)}) copy-start(bf16[1,256,2048]{2,1,0:T(8,128)(2,1)} %param.5) | copy-start | bytes 3145732
  7.2 169.9 %reduce-scatter.2.cloned.1.call-start = ((), (), s32[]{:S(2)}) async-start(), calls=%async_computation.1 | async-start | bytes 245760 | tf_op jit(solution)/shard_map/reduce_scatter | solution.py:128
  8.1 21.4 %collective-permute-start = (bf16[8,2048]{1,0:T(8,128)(2,1)S(1)}, bf16[8,2048]{1,0:T(8,128)(2,1)S(1)}, u32[]{:S(2)}, u32[]{:S(2)}) collective-permute-start(bf16[8,2048]{1,0:T(8,128)(2,1)S(1)} %slice_bitcast_fusion), channel_id=1, source_target_pairs={{0,2},{2,4},{4,6},{1,3},{3,5},{5,7},{8,10},{10,12},{12,14},{9,11},... | collective-permute-start | bytes 98312 | tf_op jit(solution)/shard_map/ppermute | solution.py:12
  36.8 1.7 copy-start
  38.6 2.3 %copy-start.4 = (f32[264,2048]{1,0:T(8,128)}, f32[264,2048]{1,0:T(8,128)S(1)}, u32[]{:S(2)}) copy-start(f32[264,2048]{1,0:T(8,128)S(1)} %get-tuple-element.50) | copy-start | bytes 6488068
  40.6 1.3 copy-start.6
  41.9 14.2 %collective-permute-start.1 = (bf16[256,2048]{1,0:T(8,128)(2,1)S(1)}, bf16[256,2048]{1,0:T(8,128)(2,1)S(1)}, u32[]{:S(2)}, u32[]{:S(2)}) collective-permute-start(bf16[256,2048]{1,0:T(8,128)(2,1)S(1)} %fusion.17), channel_id=1, source_target_pairs={{0,8},{8,16},{16,24},{24,0},{1,9},{9,17},{17,25},{25,1},{2,10},{10... | collective-permute-start | bytes 3145736 | tf_op jit(solution)/shard_map/ppermute | solution.py:18
  56.2 2.9 %collective-permute-start.2 = (bf16[8,2048]{1,0:T(8,128)(2,1)S(1)}, bf16[8,2048]{1,0:T(8,128)(2,1)S(1)}, u32[]{:S(2)}, u32[]{:S(2)}) collective-permute-start(bf16[8,2048]{1,0:T(8,128)(2,1)S(1)} %slice.239), channel_id=1, source_target_pairs={{0,2},{2,4},{4,6},{1,3},{3,5},{5,7},{8,10},{10,12},{12,14},{9,11},... | collective-permute-start | bytes 98312 | tf_op jit(solution)/shard_map/ppermute | solution.py:12
  64.7 1.4 copy-start.10
  91.5 30.6 %copy-start.5 = (f32[264,2048]{1,0:T(8,128)S(1)}, f32[264,2048]{1,0:T(8,128)}, u32[]{:S(2)}) copy-start(f32[264,2048]{1,0:T(8,128)} %copy-done.4) | copy-start | bytes 6488068
  91.5 6.6 %collective-permute-start.3 = (f32[8,2048]{1,0:T(8,128)S(1)}, f32[8,2048]{1,0:T(8,128)S(1)}, u32[]{:S(2)}, u32[]{:S(2)}) collective-permute-start(f32[8,2048]{1,0:T(8,128)S(1)} %slice.249), channel_id=1, source_target_pairs={{2,0},{4,2},{6,4},{3,1},{5,3},{7,5},{10,8},{12,10},{14,12},{11,9},... | collective-permute-start | bytes 196616 | tf_op jit(solution)/shard_map/ppermute | solution.py:12
  98.3 23.8 %collective-permute-start.4 = (f32[256,2048]{1,0:T(8,128)S(1)}, f32[256,2048]{1,0:T(8,128)S(1)}, u32[]{:S(2)}, u32[]{:S(2)}) collective-permute-start(f32[256,2048]{1,0:T(8,128)S(1)} %slice_add_fusion.1), channel_id=1, source_target_pairs={{0,24},{8,0},{16,8},{24,16},{1,25},{9,1},{17,9},{25,17},{2,26},{10... | collective-permute-start | bytes 6291464 | tf_op jit(solution)/shard_map/ppermute | solution.py:18
  122.1 9.0 %copy-start.8 = (f32[256,2048]{1,0:T(8,128)}, f32[256,2048]{1,0:T(8,128)S(1)}, u32[]{:S(2)}) copy-start(f32[256,2048]{1,0:T(8,128)S(1)} %collective-permute-done.4) | copy-start | bytes 6291460
  127.5 3.6 %copy-start.7 = (f32[264,2048]{1,0:T(8,128)S(1)}, f32[264,2048]{1,0:T(8,128)}, u32[]{:S(2)}) copy-start(f32[264,2048]{1,0:T(8,128)} %copy-done.6) | copy-start | bytes 6488068
  129.3 2.3 %copy-start.1 = (f32[264,2048]{1,0:T(8,128)S(1)}, f32[264,2048]{1,0:T(8,128)}, u32[]{:S(2)}) copy-start(f32[264,2048]{1,0:T(8,128)} %copy-done) | copy-start | bytes 6488068
  129.3 2.8 %copy-start.3 = (bf16[1,256,2048]{2,1,0:T(8,128)(2,1)S(1)}, bf16[1,256,2048]{2,1,0:T(8,128)(2,1)}, u32[]{:S(2)}) copy-start(bf16[1,256,2048]{2,1,0:T(8,128)(2,1)} %param.5) | copy-start | bytes 3145732
  140.8 7.5 %copy-start.9 = (f32[256,2048]{1,0:T(8,128)S(1)}, f32[256,2048]{1,0:T(8,128)}, u32[]{:S(2)}) copy-start(f32[256,2048]{1,0:T(8,128)} %copy-done.8) | copy-start | bytes 6291460
  140.8 7.5 %copy-start.20 = (f32[264]{0:T(512)S(1)}, f32[264]{0:T(512)}, u32[]{:S(2)}) copy-start(f32[264]{0:T(512)} %get-tuple-element.69) | copy-start | bytes 3172
  148.3 5.1 %copy-start.12 = (f32[2048]{0:T(1024)S(1)}, f32[2048]{0:T(1024)}, u32[]{:S(2)}) copy-start(f32[2048]{0:T(1024)} %get-tuple-element.12) | copy-start | bytes 24580
  148.3 5.1 %copy-start.13 = (f32[2048]{0:T(1024)S(1)}, f32[2048]{0:T(1024)}, u32[]{:S(2)}) copy-start(f32[2048]{0:T(1024)} %get-tuple-element.13) | copy-start | bytes 24580
  148.3 5.1 %copy-start.14 = (f32[2048]{0:T(1024)S(1)}, f32[2048]{0:T(1024)}, u32[]{:S(2)}) copy-start(f32[2048]{0:T(1024)} %get-tuple-element.14) | copy-start | bytes 24580
  148.4 5.1 %copy-start.15 = (f32[2048]{0:T(1024)S(1)}, f32[2048]{0:T(1024)}, u32[]{:S(2)}) copy-start(f32[2048]{0:T(1024)} %get-tuple-element.15) | copy-start | bytes 24580
  148.4 5.1 %copy-start.16 = (f32[2048]{0:T(1024)S(1)}, f32[2048]{0:T(1024)}, u32[]{:S(2)}) copy-start(f32[2048]{0:T(1024)} %get-tuple-element.16) | copy-start | bytes 24580
  148.4 5.1 %copy-start.17 = (f32[2048]{0:T(1024)S(1)}, f32[2048]{0:T(1024)}, u32[]{:S(2)}) copy-start(f32[2048]{0:T(1024)} %get-tuple-element.30) | copy-start | bytes 24580
  148.4 5.1 %copy-start.18 = (f32[2048]{0:T(1024)S(1)}, f32[2048]{0:T(1024)}, u32[]{:S(2)}) copy-start(f32[2048]{0:T(1024)} %get-tuple-element.31) | copy-start | bytes 24580
  148.4 5.1 %copy-start.19 = (f32[2048]{0:T(1024)S(1)}, f32[2048]{0:T(1024)}, u32[]{:S(2)}) copy-start(f32[2048]{0:T(1024)} %get-tuple-element.32) | copy-start | bytes 24580
  150.7 1.4 copy-start.11
  152.0 6.8 %collective-permute-start.5 = (f32[8,2048]{1,0:T(8,128)S(1)}, f32[8,2048]{1,0:T(8,128)S(1)}, u32[]{:S(2)}, u32[]{:S(2)}) collective-permute-start(f32[8,2048]{1,0:T(8,128)S(1)} %slice.251), channel_id=1, source_target_pairs={{2,0},{4,2},{6,4},{3,1},{5,3},{7,5},{10,8},{12,10},{14,12},{11,9},... | collective-permute-start | bytes 196616 | tf_op jit(solution)/shard_map/ppermute | solution.py:12
Sparse Core Ops, SparseCore 0:
  154.7 22.3 reduce-scatter.1
where the time goes:
time: 189 us; the launch traced here: 188 us
  waiting for transfers between devices  64.3 us (34%)
  other arithmetic  56.5 us (30%)
  blocking collectives  34.2 us (18%)
  between operations  14.5 us (8%)
  local copies, waits for them, and re-layouts  9.25 us (5%)
  starting transfers between devices  9.22 us (5%)
    ppermute x2, waiting for transfers between devices, shifted(): return lax.ppermute(value, axis, pairs)  37.8 us
    psum x4, blocking collectives, row_total(): return lax.psum(values, 'dp')  19.9 us
    reduce_scatter x1, waiting for transfers between devices, per_device(): lax.psum_scatter(summed_grads, 'ctx', scatter_dimension=1, tiled=True)  15.5 us
    all_gather x1, blocking collectives, per_device(): filters = lax.all_gather(packed, 'ctx', axis=1, tiled=True)  14.3 us
    reduce_sum x2, other arithmetic, conv_branch(): short_filter[tap_count * stream_index + tap_index] * lagged[tap_index]  14 us
    ppermute x4, waiting for transfers between devices, passed_along(): lax.ppermute(value, axis, [(source, source + steps) for source in range(i...  11 us
    ppermute x4, starting transfers between devices, passed_along(): lax.ppermute(value, axis, [(source, source + steps) for source in range(i...  8.9 us
    mul x12, other arithmetic, conv_branch(): mixing = mixing + long_filter[tap_index] * delayed(product, tap_index)  8.45 us
  transfers between devices with their start and end apart: 7, of which 6 were waited for; matrix products, arithmetic and copies ran while one was open for 3% of the time, Pallas kernels for 0%

commit v1 on v0

--- a/solution.py
+++ b/solution.py
@@ -42,7 +42,7 @@
 
 
 def row_total(values):
-    return lax.psum(values, "dp")
+    return jnp.sum(lax.all_gather(values, "dp"), axis=0)
 
 
 def block_forward(values, filter_set):

time: 189 us -> 192 us (1.016)
  local copies, waits for them, and re-layouts: 9.25 us -> 11.7 us
    psum x4 -> x0, blocking collectives: 19.9 us -> none  [row_total(): return lax.psum(values, 'dp')]
    unnamed x0 -> x4, blocking collectives: none -> 19.7 us
    unnamed x44 -> x53, local copies, waits for them, and re-layouts: 4.21 us -> 6.37 us
  transfers between devices with their start and end apart: 7 -> 7, of which waited for: 6 -> 6; matrix products, arithmetic and copies ran while one was open for 3% -> 4% of each run, Pallas kernels for 0% -> 0%
where the time goes in v1:
time: 192 us; the launch traced here: 191 us
  waiting for transfers between devices  64.3 us (33%)
  other arithmetic  56.7 us (30%)
  blocking collectives  33.9 us (18%)
  between operations  15.2 us (8%)
  local copies, waits for them, and re-layouts  11.7 us (6%)
  starting transfers between devices  9.22 us (5%)
    ppermute x2, waiting for transfers between devices, shifted(): return lax.ppermute(value, axis, pairs)  37.8 us
    unnamed x4, blocking collectives  19.7 us
    reduce_scatter x1, waiting for transfers between devices, per_device(): lax.psum_scatter(summed_grads, 'ctx', scatter_dimension=1, tiled=True)  15.5 us
    all_gather x1, blocking collectives, per_device(): filters = lax.all_gather(packed, 'ctx', axis=1, tiled=True)  14.3 us
    reduce_sum x2, other arithmetic, conv_branch(): short_filter[tap_count * stream_index + tap_index] * lagged[tap_index]  14 us
    ppermute x4, waiting for transfers between devices, passed_along(): lax.ppermute(value, axis, [(source, source + steps) for source in range(i...  11 us
    ppermute x4, starting transfers between devices, passed_along(): lax.ppermute(value, axis, [(source, source + steps) for source in range(i...  8.9 us
    mul x12, other arithmetic, conv_branch(): mixing = mixing + long_filter[tap_index] * delayed(product, tap_index)  8.45 us
  transfers between devices with their start and end apart: 7, of which 6 were waited for; matrix products, arithmetic and copies ran while one was open for 4% of the time, Pallas kernels for 0%

profile of v1, /device:TPU:0, one launch (start us, length us, event | category | flops | bytes accessed | tf_op | source)
XLA Modules:
  0.0 191.1 jit_solution(9225880144457772900)
XLA Ops:
  7.2 0.8 slice_bitcast_fusion
  8.1 4.9 %collective-permute-start = (bf16[8,2048]{1,0:T(8,128)(2,1)S(1)}, bf16[8,2048]{1,0:T(8,128)(2,1)S(1)}, u32[]{:S(2)}, u32[]{:S(2)}) collective-permute-start(bf16[8,2048]{1,0:T(8,128)(2,1)S(1)} %slice_bitcast_fusion), channel_id=1, source_target_pairs={{0,2},{2,4},{4,6},{1,3},{3,5},{5,7},{8,10},{10,12},{12,14},{9,11},... | collective-permute-start | bytes 98312 | tf_op jit(solution)/shard_map/ppermute | solution.py:12
  13.0 0.7 copy.13
  13.7 0.7 copy.14
  14.4 0.7 pad_maximum_fusion.2
  15.1 14.3 %all_gather.27 = f32[17,2048]{1,0:T(8,128)S(1)} all-gather(f32[17,512]{1,0:T(8,128)S(1)} %pad_maximum_fusion.2), channel_id=1, replica_groups=mesh['pipe'=4,'ctx'=4,'dp'=2] {'ctx'}, dimensions={1}, use_global_device_ids=true | all-gather | bytes 174080 | tf_op jit(solution)/shard_map/all_gather | solution.py:108
  29.5 1.2 dynamic-slice
  31.4 1.5 multiply_reduce_fusion.34
  33.2 4.9 %all-reduce.68 = f32[528]{0:T(1024)S(1)} all-reduce(f32[528]{0:T(1024)S(1)} %dynamic-update-slice), channel_id=2, replica_groups=mesh['pipe'=4,'ctx'=4,'dp'=2] {'dp'}, use_global_device_ids=true, to_apply=%add.68 | all-reduce | flops 528 | bytes 4224
  39.1 1.7 multiply_add_fusion.7
  40.8 2.0 %multiply_add_fusion.4 = f32[264,2048]{1,0:T(8,128)S(1)} fusion(f32[264,2048]{1,0:T(8,128)S(1)} %get-tuple-element.51, f32[258,2048]{1,0:T(8,128)S(1)} %bitcast.92, f32[259,2048]{1,0:T(8,128)S(1)} %bitcast.93, f32[260,2048]{1,0:T(8,128)S(1)} %bitcast.94, f32[261,2048]{1,0:T(8,128)S(1)} %bitcast.95, f32[262,2048]{1,0:T(8,128)S(1)} %bitcast.96, ...), kind=kLoop, calls=%fused_computation.87 | loop fusion | flops 7028736 | bytes 17186816 | tf_op jit(solution)/shard_map/jvp()/add | solution.py:40
  43.1 0.6 fusion.17
  44.2 14.2 %collective-permute-done.1 = bf16[256,2048]{1,0:T(8,128)(2,1)S(1)} collective-permute-done((bf16[256,2048]{1,0:T(8,128)(2,1)S(1)}, bf16[256,2048]{1,0:T(8,128)(2,1)S(1)}, u32[]{:S(2)}, u32[]{:S(2)}) %collective-permute-start.1) | collective-permute-done | bytes 1048608 | tf_op jit(solution)/shard_map/ppermute | solution.py:18
  58.4 1.3 collective-permute-start.2
  59.7 1.6 collective-permute-done.2
  61.8 4.9 %all-reduce.69 = f32[528]{0:T(1024)S(1)} all-reduce(f32[528]{0:T(1024)S(1)} %dynamic-update-slice.1), channel_id=3, replica_groups=mesh['pipe'=4,'ctx'=4,'dp'=2] {'dp'}, use_global_device_ids=true, to_apply=%add.69 | all-reduce | flops 528 | bytes 4224
  67.2 1.4 fusion.24
  68.5 4.7 %multiply_reduce_fusion.6 = (f32[2048]{0:T(1024)S(1)}, f32[2048]{0:T(1024)S(1)}, f32[2048]{0:T(1024)S(1)}, f32[2048]{0:T(1024)S(1)}, f32[2048]{0:T(1024)S(1)}, /...) fusion(f32[258,2048]{1,0:T(8,128)S(1)} %bitcast.80, f32[264,2048]{1,0:T(8,128)S(1)} %fusion.24, ...), kind=kLoop, calls=%fused_computation.52 | loop fusion | flops 14583808 | bytes 23651360 | tf_op jit(solution)/shard_map/transpose(jvp())/reduce_sum | solution.py:40
  75.4 6.8 %multiply_reduce_fusion.15 = (f32[2048]{0:T(1024)S(1)}, f32[2048]{0:T(1024)S(1)}, f32[2048]{0:T(1024)S(1)}, f32[2048]{0:T(1024)S(1)}, f32[2048]{0:T(1024)}, /*in...) fusion(f32[262,2048]{1,0:T(8,128)S(1)} %bitcast.108, ...), kind=kLoop, calls=%fused_computation.61 | loop fusion | flops 31340544 | bytes 43041824 | tf_op jit(solution)/shard_map/transpose(jvp())/reduce_sum | solution.py:35
  82.2 0.8 fusion.13
  83.0 0.9 fusion.11
  83.9 2.6 %fusion.2 = (f32[2048]{0:T(1024)S(1)}, f32[264]{0:T(512)S(1)}, f32[264,2048]{1,0:T(8,128)}) fusion(f32[264]{0:T(512)S(1)} %get-tuple-element.72, bf16[256,2048]{1,0:T(8,128)(2,1)S(1)} %collective-permute-done.1, bf16[8,2048]{1,0:T(8,128)(2,1)S(1)} %collective-permute-done.2, f32[2048]{0:T(1024)S(1)} %bitcast.130, f32[263,2048]{1,0:T(8,128)S(1)} %fusion.11, ...), kind=kLoop, calls=%fused_computation.9 | loop fusion | flops 9189112 | bytes 14075968 | tf_op jit(solution)/shard_map/reduce_sum | solution.py:59
  86.7 4.9 %all-reduce.70 = f32[528]{0:T(1024)S(1)} all-reduce(f32[528]{0:T(1024)S(1)} %dynamic-update-slice.2), channel_id=4, replica_groups=mesh['pipe'=4,'ctx'=4,'dp'=2] {'dp'}, use_global_device_ids=true, to_apply=%add.70 | all-reduce | flops 528 | bytes 4224
  91.7 2.5 %fusion.3 = f32[264,2048]{1,0:T(8,128)S(1)} fusion(f32[264,2048]{1,0:T(8,128)} %get-tuple-element.49, f32[264]{0:T(512)S(1)} %reduce_sum.377, f32[264]{0:T(512)S(1)} %get-tuple-element.71, f32[264]{0:T(512)S(1)} %get-tuple-element.72, f32[2048]{0:T(1024)S(1)} %bitcast.131, bf16[256,2048]{1,0:T(8,128)(2,1)} %bitcast.121, ...), kind=kLoop, calls=%fused_computation.10 | loop fusion | flops 5947392 | bytes 6466656 | tf_op jit(solution)/shard_map/sub | solution.py:62
  94.3 1.4 collective-permute-start.3
  95.7 5.2 %collective-permute-done.3 = f32[8,2048]{1,0:T(8,128)S(1)} collective-permute-done((f32[8,2048]{1,0:T(8,128)S(1)}, f32[8,2048]{1,0:T(8,128)S(1)}, u32[]{:S(2)}, u32[]{:S(2)}) %collective-permute-start.3) | collective-permute-done | bytes 65568 | tf_op jit(solution)/shard_map/ppermute | solution.py:12
  101.3 23.5 %collective-permute-done.4 = f32[256,2048]{1,0:T(8,128)S(1)} collective-permute-done((f32[256,2048]{1,0:T(8,128)S(1)}, f32[256,2048]{1,0:T(8,128)S(1)}, u32[]{:S(2)}, u32[]{:S(2)}) %collective-permute-start.4) | collective-permute-done | bytes 2097184 | tf_op jit(solution)/shard_map/ppermute | solution.py:18
  124.9 2.6 %multiply_reduce_fusion.22 = (f32[2048]{0:T(1024)S(1)}, f32[2048]{0:T(1024)S(1)}, f32[2048]{0:T(1024)S(1)}, f32[2048]{0:T(1024)S(1)}, f32[2048]{0:T(1024)S(1)}, ...) fusion(f32[258,2048]{1,0:T(8,128)S(1)} %bitcast.98, f32[264,2048]{1,0:T(8,128)S(1)} %get-tuple-element.51, ...), kind=kLoop, calls=%fused_computation.68 | loop fusion | flops 8095744 | bytes 21446656 | tf_op jit(solution)/shard_map/transpose(jvp())/reduce_sum | solution.py:40
  128.5 1.8 slice_multiply_fusion.8
  130.3 1.8 slice_multiply_fusion.9
  132.1 1.8 slice_multiply_fusion.6
  134.9 7.2 %multiply_reduce_fusion.31 = (f32[2048]{0:T(1024)S(1)}, f32[2048]{0:T(1024)S(1)}, f32[2048]{0:T(1024)S(1)}, f32[2048]{0:T(1024)S(1)}, f32[2048]{0:T(1024)S(1)}, ...) fusion(f32[262,2048]{1,0:T(8,128)S(1)} %bitcast.112, ...), kind=kLoop, calls=%fused_computation.77 | loop fusion | flops 23771136 | bytes 31237152 | tf_op jit(solution)/shard_map/transpose(jvp())/reduce_sum | solution.py:35
  142.0 0.8 fusion.9
  142.8 0.8 fusion.7
  143.7 2.6 %multiply_reduce_fusion.32 = (f32[2048]{0:T(1024)S(1)}, f32[264]{0:T(512)S(1)}, f32[264,2048]{1,0:T(8,128)}) fusion(f32[264]{0:T(512)S(1)} %get-tuple-element.70, bf16[256,2048]{1,0:T(8,128)(2,1)S(1)} %bitcast.119, bf16[8,2048]{1,0:T(8,128)(2,1)S(1)} %collective-permute-done, f32[2048]{0:T(1024)S(1)} %bitcast.133, f32[263,2048]{1,0:T(8,128)S(1)} %fusion.7, ...), kind=kLoop, calls=%fused_computation.78 | loop fusion | flops 9189112 | bytes 14075968 | tf_op jit(solution)/shard_map/reduce_sum | solution.py:59
  146.4 4.9 %all-reduce.71 = f32[528]{0:T(1024)S(1)} all-reduce(f32[528]{0:T(1024)S(1)} %dynamic-update-slice.3), channel_id=5, replica_groups=mesh['pipe'=4,'ctx'=4,'dp'=2] {'dp'}, use_global_device_ids=true, to_apply=%add.71 | all-reduce | flops 528 | bytes 4224
  151.5 2.3 %multiply_subtract_fusion = f32[264,2048]{1,0:T(8,128)S(1)} fusion(f32[264,2048]{1,0:T(8,128)} %get-tuple-element.48, f32[256,2048]{1,0:T(8,128)S(1)} %copy-done.9, f32[264]{0:T(512)S(1)} %reduce_sum.379, f32[264]{0:T(512)S(1)} %copy-done.20, f32[2048]{0:T(1024)S(1)} %bitcast.134, f32[264]{0:T(512)S(1)} %get-tuple-element.70, ...), kind=kLoop, calls=%fused_computation.79 | loop fusion | flops 5406720 | bytes 7515232 | tf_op jit(solution)/shard_map/sub | solution.py:62
  153.8 1.3 copy-done.11
  155.2 1.3 collective-permute-start.5
  156.9 0.8 maximum_add_fusion
  157.7 4.3 %collective-permute-done.5 = f32[8,2048]{1,0:T(8,128)S(1)} collective-permute-done((f32[8,2048]{1,0:T(8,128)S(1)}, f32[8,2048]{1,0:T(8,128)S(1)}, u32[]{:S(2)}, u32[]{:S(2)}) %collective-permute-start.5) | collective-permute-done | bytes 65568 | tf_op jit(solution)/shard_map/ppermute | solution.py:12
  162.0 2.7 %fusion.18 = bf16[1,256,2048]{2,1,0:T(8,128)(2,1)} fusion(f32[8,2048]{1,0:T(8,128)S(1)} %collective-permute-done.5, f32[264,2048]{1,0:T(8,128)} %copy-done.11), kind=kLoop, calls=%fused_computation.104 | loop fusion | flops 1048576 | bytes 3211264 | tf_op jit(solution)/shard_map/broadcast_in_dim | solution.py:132
  164.7 15.5 %reduce-scatter.2.cloned.1.call-done = f32[17,512]{1,0:T(8,128)} async-done(((f32[17,2048]{1,0:T(8,128)}), f32[17,512]{1,0:T(8,128)}) %reduce-scatter.2.cloned.1.call-update) | async-done | bytes 34832 | tf_op jit(solution)/shard_map/reduce_scatter | solution.py:128
  180.2 0.8 slice.253
  181.0 0.6 broadcast_in_dim.13
  181.6 0.8 slice.254
  182.4 0.6 broadcast_in_dim.14
  183.0 1.3 slice.252
  (84 shorter events, 8.5 us)
Async XLA Ops:
  7.2 31.6 %copy-start.2 = (bf16[1,256,2048]{2,1,0:T(8,128)(2,1)S(1)}, bf16[1,256,2048]{2,1,0:T(8,128)(2,1)}, u32[]{:S(2)}) copy-start(bf16[1,256,2048]{2,1,0:T(8,128)(2,1)} %param.5) | copy-start | bytes 3145732
  7.2 173.0 %reduce-scatter.2.cloned.1.call-start = ((), (), s32[]{:S(2)}) async-start(), calls=%async_computation.1 | async-start | bytes 245760 | tf_op jit(solution)/shard_map/reduce_scatter | solution.py:128
  8.1 23.3 %collective-permute-start = (bf16[8,2048]{1,0:T(8,128)(2,1)S(1)}, bf16[8,2048]{1,0:T(8,128)(2,1)S(1)}, u32[]{:S(2)}, u32[]{:S(2)}) collective-permute-start(bf16[8,2048]{1,0:T(8,128)(2,1)S(1)} %slice_bitcast_fusion), channel_id=1, source_target_pairs={{0,2},{2,4},{4,6},{1,3},{3,5},{5,7},{8,10},{10,12},{12,14},{9,11},... | collective-permute-start | bytes 98312 | tf_op jit(solution)/shard_map/ppermute | solution.py:12
  39.1 1.7 copy-start
  40.8 2.3 %copy-start.4 = (f32[264,2048]{1,0:T(8,128)}, f32[264,2048]{1,0:T(8,128)S(1)}, u32[]{:S(2)}) copy-start(f32[264,2048]{1,0:T(8,128)S(1)} %get-tuple-element.50) | copy-start | bytes 6488068
  42.8 1.3 copy-start.6
  44.2 14.2 %collective-permute-start.1 = (bf16[256,2048]{1,0:T(8,128)(2,1)S(1)}, bf16[256,2048]{1,0:T(8,128)(2,1)S(1)}, u32[]{:S(2)}, u32[]{:S(2)}) collective-permute-start(bf16[256,2048]{1,0:T(8,128)(2,1)S(1)} %fusion.17), channel_id=1, source_target_pairs={{0,8},{8,16},{16,24},{24,0},{1,9},{9,17},{17,25},{25,1},{2,10},{10... | collective-permute-start | bytes 3145736 | tf_op jit(solution)/shard_map/ppermute | solution.py:18
  58.4 2.9 %collective-permute-start.2 = (bf16[8,2048]{1,0:T(8,128)(2,1)S(1)}, bf16[8,2048]{1,0:T(8,128)(2,1)S(1)}, u32[]{:S(2)}, u32[]{:S(2)}) collective-permute-start(bf16[8,2048]{1,0:T(8,128)(2,1)S(1)} %slice.239), channel_id=1, source_target_pairs={{0,2},{2,4},{4,6},{1,3},{3,5},{5,7},{8,10},{10,12},{12,14},{9,11},... | collective-permute-start | bytes 98312 | tf_op jit(solution)/shard_map/ppermute | solution.py:12
  67.1 1.4 copy-start.10
  94.2 30.6 %copy-start.5 = (f32[264,2048]{1,0:T(8,128)S(1)}, f32[264,2048]{1,0:T(8,128)}, u32[]{:S(2)}) copy-start(f32[264,2048]{1,0:T(8,128)} %copy-done.4) | copy-start | bytes 6488068
  94.3 6.6 %collective-permute-start.3 = (f32[8,2048]{1,0:T(8,128)S(1)}, f32[8,2048]{1,0:T(8,128)S(1)}, u32[]{:S(2)}, u32[]{:S(2)}) collective-permute-start(f32[8,2048]{1,0:T(8,128)S(1)} %slice.249), channel_id=1, source_target_pairs={{2,0},{4,2},{6,4},{3,1},{5,3},{7,5},{10,8},{12,10},{14,12},{11,9},... | collective-permute-start | bytes 196616 | tf_op jit(solution)/shard_map/ppermute | solution.py:12
  101.0 23.8 %collective-permute-start.4 = (f32[256,2048]{1,0:T(8,128)S(1)}, f32[256,2048]{1,0:T(8,128)S(1)}, u32[]{:S(2)}, u32[]{:S(2)}) collective-permute-start(f32[256,2048]{1,0:T(8,128)S(1)} %slice_add_fusion.1), channel_id=1, source_target_pairs={{0,24},{8,0},{16,8},{24,16},{1,25},{9,1},{17,9},{25,17},{2,26},{10... | collective-permute-start | bytes 6291464 | tf_op jit(solution)/shard_map/ppermute | solution.py:18
  124.9 9.0 %copy-start.8 = (f32[256,2048]{1,0:T(8,128)}, f32[256,2048]{1,0:T(8,128)S(1)}, u32[]{:S(2)}) copy-start(f32[256,2048]{1,0:T(8,128)S(1)} %collective-permute-done.4) | copy-start | bytes 6291460
  130.3 3.6 %copy-start.7 = (f32[264,2048]{1,0:T(8,128)S(1)}, f32[264,2048]{1,0:T(8,128)}, u32[]{:S(2)}) copy-start(f32[264,2048]{1,0:T(8,128)} %copy-done.6) | copy-start | bytes 6488068
  132.1 2.2 %copy-start.1 = (f32[264,2048]{1,0:T(8,128)S(1)}, f32[264,2048]{1,0:T(8,128)}, u32[]{:S(2)}) copy-start(f32[264,2048]{1,0:T(8,128)} %copy-done) | copy-start | bytes 6488068
  132.1 2.7 %copy-start.3 = (bf16[1,256,2048]{2,1,0:T(8,128)(2,1)S(1)}, bf16[1,256,2048]{2,1,0:T(8,128)(2,1)}, u32[]{:S(2)}) copy-start(bf16[1,256,2048]{2,1,0:T(8,128)(2,1)} %param.5) | copy-start | bytes 3145732
  143.7 7.8 %copy-start.9 = (f32[256,2048]{1,0:T(8,128)S(1)}, f32[256,2048]{1,0:T(8,128)}, u32[]{:S(2)}) copy-start(f32[256,2048]{1,0:T(8,128)} %copy-done.8) | copy-start | bytes 6291460
  143.7 7.8 %copy-start.20 = (f32[264]{0:T(512)S(1)}, f32[264]{0:T(512)}, u32[]{:S(2)}) copy-start(f32[264]{0:T(512)} %get-tuple-element.69) | copy-start | bytes 3172
  151.4 5.1 %copy-start.12 = (f32[2048]{0:T(1024)S(1)}, f32[2048]{0:T(1024)}, u32[]{:S(2)}) copy-start(f32[2048]{0:T(1024)} %get-tuple-element.12) | copy-start | bytes 24580
  151.5 5.1 %copy-start.13 = (f32[2048]{0:T(1024)S(1)}, f32[2048]{0:T(1024)}, u32[]{:S(2)}) copy-start(f32[2048]{0:T(1024)} %get-tuple-element.13) | copy-start | bytes 24580
  151.5 5.1 %copy-start.14 = (f32[2048]{0:T(1024)S(1)}, f32[2048]{0:T(1024)}, u32[]{:S(2)}) copy-start(f32[2048]{0:T(1024)} %get-tuple-element.14) | copy-start | bytes 24580
  151.5 5.1 %copy-start.15 = (f32[2048]{0:T(1024)S(1)}, f32[2048]{0:T(1024)}, u32[]{:S(2)}) copy-start(f32[2048]{0:T(1024)} %get-tuple-element.15) | copy-start | bytes 24580
  151.5 5.1 %copy-start.16 = (f32[2048]{0:T(1024)S(1)}, f32[2048]{0:T(1024)}, u32[]{:S(2)}) copy-start(f32[2048]{0:T(1024)} %get-tuple-element.16) | copy-start | bytes 24580
  151.5 5.1 %copy-start.17 = (f32[2048]{0:T(1024)S(1)}, f32[2048]{0:T(1024)}, u32[]{:S(2)}) copy-start(f32[2048]{0:T(1024)} %get-tuple-element.30) | copy-start | bytes 24580
  151.5 5.1 %copy-start.18 = (f32[2048]{0:T(1024)S(1)}, f32[2048]{0:T(1024)}, u32[]{:S(2)}) copy-start(f32[2048]{0:T(1024)} %get-tuple-element.31) | copy-start | bytes 24580
  151.5 5.1 %copy-start.19 = (f32[2048]{0:T(1024)S(1)}, f32[2048]{0:T(1024)}, u32[]{:S(2)}) copy-start(f32[2048]{0:T(1024)} %get-tuple-element.32) | copy-start | bytes 24580
  153.8 1.4 copy-start.11
  155.2 6.8 %collective-permute-start.5 = (f32[8,2048]{1,0:T(8,128)S(1)}, f32[8,2048]{1,0:T(8,128)S(1)}, u32[]{:S(2)}, u32[]{:S(2)}) collective-permute-start(f32[8,2048]{1,0:T(8,128)S(1)} %slice.251), channel_id=1, source_target_pairs={{2,0},{4,2},{6,4},{3,1},{5,3},{7,5},{10,8},{12,10},{14,12},{11,9},... | collective-permute-start | bytes 196616 | tf_op jit(solution)/shard_map/ppermute | solution.py:12
Sparse Core Ops, SparseCore 0:
  157.8 22.3 reduce-scatter.1
